TPU v7x, 256 devices: a whole 4x4x8 slice. The times are simulated.
256 devices in a mesh: fsdp: 16 (over y, z_hi), seq: 16 (over x, z_lo, core).
Axes of the slice: x: 4, y: 4, z: 8 (z_hi: 4, z_lo: 2; z = z_hi * 2 + z_lo), core: 2. Of those that a mesh axis runs over, the one named last changes fastest.
Arguments:
- hidden: bfloat16 [16, 2048, 5120], P('fsdp', 'seq'), may hold values from -6 to 6
- queries: bfloat16 [16, 2048, 4096], P('fsdp', 'seq'), may hold values from -400 to 400
- key_value_weight: bfloat16 [5120, 2048], P('fsdp'), may hold values from -0.078125 to 0.078125
- doc_lengths: int32 [16, 16], P('fsdp'), may hold values from 1 to 1024, 2048 in all within a row
- resp_lengths: int32 [16, 16], P('fsdp'), may hold values from 1 to 128
Outputs:
- attended: bfloat16 [16, 2048, 4096], P('fsdp', 'seq')
- pooled: float32 [16, 16, 4096], P('fsdp', None, 'seq')
Inputs may be any that keep to these rules, and one draw needn't show every extreme that they name: `doc_lengths`: each row holds the lengths of the documents of one packed sequence in order; they sum to 2048 and the longest is exactly 1024.
All inputs are finite; a program needn't handle non-finite values.
Results may differ from a plain program's by a relative error of at most 0.011.
Values may be sent and summed in bfloat16 or wider, within the bound.
No kernel may reach another device: no remote copies, remote signals or barrier semaphores. Data moves between devices by JAX's collectives and lax.ppermute only.
A program may use at most 128 MiB of HBM per device.

v0:
```python
import jax
import jax.numpy as jnp
from jax import lax
from jax.sharding import PartitionSpec as P

HEAD_SIZE = 128
KEY_VALUE_HEADS = 8
ROPE_BASE = 1000000.0


def token_tables(lengths, wanted, first, count):
    ends = jnp.cumsum(lengths)
    starts = ends - lengths
    answer = jnp.minimum(wanted, lengths)
    index = first + jnp.arange(count, dtype=jnp.int32)
    inside = (index[:, None] >= starts[None, :]) & (index[:, None] < ends[None, :])
    token_position = jnp.sum(jnp.where(inside, index[:, None] - starts[None, :], 0), axis=1)
    doc_id = jnp.sum(jnp.where(index[:, None] >= ends[None, :], 1, 0), axis=1).astype(jnp.int32)
    member = jnp.where(inside & (index[:, None] >= (ends - answer)[None, :]), 1, 0).astype(
        jnp.int32
    )
    return (token_position, doc_id, member, answer)


def rotate_pairs(heads, token_position):
    half = heads.shape[-1] // 2
    freq = ROPE_BASE ** (-(jnp.arange(half, dtype=jnp.float32) * 2.0 / heads.shape[-1]))
    angle = token_position.astype(jnp.float32)[:, None] * freq[None, :]
    cosine = jnp.cos(angle)[:, None, :]
    sine = jnp.sin(angle)[:, None, :]
    first = heads[..., :half]
    second = heads[..., half:]
    return jnp.concatenate(
        [first * cosine - second * sine, second * cosine + first * sine], axis=-1
    )


def on_device(hidden, queries, key_value_weight, doc_lengths, resp_lengths):
    piece_list = lax.axis_size("seq")
    rank = lax.axis_index("seq")
    token_batch = hidden.shape[1]
    length = token_batch * piece_list
    longest = length // 2
    kv_cols = key_value_weight.shape[1]
    key_value_split = kv_cols // 2
    lengths = doc_lengths[0]
    wanted = resp_lengths[0]
    features = hidden[0]
    projected_rows = jnp.dot(
        features,
        lax.all_gather(key_value_weight, "fsdp", axis=0, tiled=True),
        preferred_element_type=jnp.float32,
    )
    local_tables = token_tables(lengths, wanted, rank * token_batch, token_batch)
    key_rows = rotate_pairs(
        projected_rows[:, :key_value_split].reshape(token_batch, KEY_VALUE_HEADS, HEAD_SIZE),
        local_tables[0],
    ).astype(jnp.bfloat16)
    value_rows = (
        projected_rows[:, key_value_split:]
        .reshape(token_batch, KEY_VALUE_HEADS, HEAD_SIZE)
        .astype(jnp.bfloat16)
    )
    repeat_heads = max(1, piece_list // KEY_VALUE_HEADS)
    key_rows = jnp.broadcast_to(
        key_rows[:, :, None, :], (token_batch, KEY_VALUE_HEADS, repeat_heads, HEAD_SIZE)
    ).reshape(1, token_batch, KEY_VALUE_HEADS * repeat_heads * HEAD_SIZE)
    value_rows = jnp.broadcast_to(
        value_rows[:, :, None, :], (token_batch, KEY_VALUE_HEADS, repeat_heads, HEAD_SIZE)
    ).reshape(1, token_batch, KEY_VALUE_HEADS * repeat_heads * HEAD_SIZE)
    q_heads, k_heads, v_heads = (
        lax.all_to_all(queries, "seq", split_axis=2, concat_axis=1, tiled=True),
        lax.all_to_all(key_rows, "seq", split_axis=2, concat_axis=1, tiled=True),
        lax.all_to_all(value_rows, "seq", split_axis=2, concat_axis=1, tiled=True),
    )
    q_count = q_heads.shape[2] // HEAD_SIZE
    kv_count = k_heads.shape[2] // HEAD_SIZE
    query_group = q_count // kv_count
    all_tables = token_tables(lengths, wanted, jnp.int32(0), length)
    doc_id = all_tables[1]
    answer = all_tables[3]
    query_matrix = q_heads[0].reshape(length, kv_count, query_group, HEAD_SIZE)
    key_all = k_heads[0].reshape(length, kv_count, HEAD_SIZE)
    value_all = v_heads[0].reshape(length, kv_count, HEAD_SIZE)
    block = min(512, length)
    window = min(length, block + longest)

    def attend(index):
        qstart = index * block
        kstart = jnp.maximum(qstart + block - window, 0)
        qblock = lax.dynamic_slice_in_dim(query_matrix, qstart, block, 0)
        kblock = lax.dynamic_slice_in_dim(key_all, kstart, window, 0)
        vblock = lax.dynamic_slice_in_dim(value_all, kstart, window, 0)
        qdoc = lax.dynamic_slice_in_dim(doc_id, qstart, block, 0)
        kdoc = lax.dynamic_slice_in_dim(doc_id, kstart, window, 0)
        qplace = qstart + jnp.arange(block, dtype=jnp.int32)
        kplace = kstart + jnp.arange(window, dtype=jnp.int32)
        allowed = (qdoc[:, None] == kdoc[None, :]) & (kplace[None, :] <= qplace[:, None])
        scores = jnp.einsum(
            "qkgd,skd->kgqs", qblock, kblock, preferred_element_type=jnp.float32
        ) * HEAD_SIZE ** (-0.5)
        scores = jnp.where(allowed, scores, -1e30)
        peak = jnp.max(scores, axis=-1, keepdims=True)
        weight = jnp.where(allowed, jnp.exp(scores - peak), 0.0)
        probs = (weight / jnp.sum(weight, axis=-1, keepdims=True)).astype(jnp.bfloat16)
        output = jnp.einsum("kgqs,skd->qkgd", probs, vblock, preferred_element_type=jnp.float32)
        return output.astype(jnp.bfloat16).reshape(block, q_count * HEAD_SIZE)

    attn_heads = lax.map(attend, jnp.arange(length // block, dtype=jnp.int32)).reshape(
        length, q_count * HEAD_SIZE
    )
    attended = lax.all_to_all(attn_heads[None], "seq", split_axis=1, concat_axis=2, tiled=True)
    partial_value = jnp.einsum(
        "tr,tc->rc",
        local_tables[2].astype(jnp.bfloat16),
        attended[0],
        preferred_element_type=jnp.float32,
    )
    sums = lax.psum_scatter(
        partial_value.astype(jnp.bfloat16), "seq", scatter_dimension=1, tiled=True
    ).astype(jnp.float32)
    pooled = sums / answer.astype(jnp.float32)[:, None]
    return (attended, pooled[None])


def solution(mesh):
    in_specs = (
        P("fsdp", "seq", None),
        P("fsdp", "seq", None),
        P("fsdp", None),
        P("fsdp", None),
        P("fsdp", None),
    )
    out_specs = (P("fsdp", "seq", None), P("fsdp", None, "seq"))
    return jax.shard_map(
        on_device, mesh=mesh, in_specs=in_specs, out_specs=out_specs, check_vma=False
    )
```

profile of v0, /device:TPU:8, one launch (start us, length us, event | category | flops | bytes accessed | tf_op | source)
XLA Modules:
  0.0 494.3 jit_solution(4194151677751714912)
XLA Ops:
  7.2 0.7 all-gather.2.cloned.1.call-update
  7.9 5.0 %copy.69 = bf16[1,128,4096]{1,0,2:T(2,128)(2,1)S(1)} copy(bf16[1,128,4096]{2,1,0:T(8,128)(2,1)} %param.8) | data formatting | bytes 2097152 | tf_op args[1]
  13.0 0.5 broadcast.95
  13.5 23.4 %reduce.18 = bf16[4096,128]{1,0:T(8,128)(2,1)} reduce(bf16[4096,1,128]{2,1,0:T(2,128)(2,1)S(1)} %bitcast.129, bf16[]{:T(256)} %broadcast.95), dimensions={1}, to_apply=%bitcast.91.reduce_sub_computation | reduce | bytes 2097154
  36.9 2.1 reshape.212
  39.0 6.2 %all-to-all-start.2 = ((bf16[16,2,16384]{2,1,0:T(2,128)(2,1)}), bf16[16,2,16384]{2,1,0:T(2,128)(2,1)S(1)}, u32[]{:S(2)}, u32[]{:S(2)}) async-start(bf16[16,2,16384]{2,1,0:T(2,128)(2,1)} %reshape.212), calls=%async_computation.2 | async-start | bytes 2097152 | tf_op jit(solution)/shard_map/all_to_all | solution.py:72
  45.5 0.6 convert_bitcast_fusion
  46.2 0.3 multiply_cosine_fusion
  46.5 221.5 %all-gather.2.cloned.1.call-done = bf16[5120,2048]{1,0:T(8,128)(2,1)} async-done(((bf16[320,2048]{1,0:T(8,128)(2,1)}), bf16[5120,2048]{1,0:T(8,128)(2,1)}) %all-gather.2.cloned.1.call-update) | async-done | bytes 20971536 | tf_op jit(solution)/shard_map/all_gather | solution.py:51
  268.0 8.5 %fusion.19 = f32[128,2048]{1,0:T(8,128)S(1)} fusion(bf16[5120,2048]{1,0:T(8,128)(2,1)} %all-gather.2.cloned.1.call-done, bf16[1,128,5120]{2,1,0:T(8,128)(2,1)S(1)} %copy-done), kind=kOutput, calls=%fused_computation.25 | convolution fusion | flops 2684354560 | bytes 23330816 | tf_op jit(solution)/shard_map/dot_general | solution.py:49
  276.6 0.3 subtract_convert_fusion
  276.9 0.1 pad_maximum_fusion
  277.1 0.2 copy.66
  277.4 8.1 %copy.93 = bf16[1,128,2048]{1,0,2:T(2,128)(2,1)S(1)} copy(bf16[1,128,2048]{1,2,0:T(8,128)(2,1)S(1)} %bitcast.139) | data formatting | bytes 1048576 | tf_op jit(solution)/shard_map/reshape | solution.py:67
  285.6 12.3 %reduce.17 = bf16[2048,128]{1,0:T(8,128)(2,1)} reduce(bf16[2048,1,128]{2,1,0:T(2,128)(2,1)S(1)} %bitcast.137, bf16[]{:T(256)} %broadcast.95), dimensions={1}, to_apply=%bitcast.105.reduce_sub_computation | reduce | bytes 1048578
  297.9 2.0 reshape.210
  299.8 4.4 all-to-all-start.1
  304.3 0.2 copy.79
  304.6 8.1 %copy.94 = bf16[1,128,2048]{1,0,2:T(2,128)(2,1)S(1)} copy(bf16[1,128,2048]{1,2,0:T(8,128)(2,1)S(1)} %bitcast.140) | data formatting | bytes 1048576 | tf_op jit(solution)/shard_map/reshape | solution.py:70
  312.7 11.5 %reduce.16 = bf16[2048,128]{1,0:T(8,128)(2,1)S(1)} reduce(bf16[2048,1,128]{2,1,0:T(2,128)(2,1)S(1)} %bitcast.138, bf16[]{:T(256)} %broadcast.95), dimensions={1}, to_apply=%bitcast.106.reduce_sub_computation | reduce | bytes 1048578
  324.2 0.9 reshape.208
  325.2 5.6 %all-to-all-start = ((bf16[16,2,8192]{2,1,0:T(2,128)(2,1)}), bf16[16,2,8192]{2,1,0:T(2,128)(2,1)}, u32[]{:S(2)}, u32[]{:S(2)}) async-start(bf16[16,2,8192]{2,1,0:T(2,128)(2,1)} %reshape.208), calls=%async_computation | async-start | bytes 1048576 | tf_op jit(solution)/shard_map/all_to_all | solution.py:74
  330.8 0.3 reduce-scatter.2.cloned.1.call-start
  331.2 4.3 reshape.213
  335.7 0.7 copy.70
  336.3 1.3 reshape_squeeze.11
  337.6 2.2 reshape.211
  339.9 0.3 copy.68
  340.2 1.5 all-to-all-done
  341.7 2.2 reshape.209
  344.0 1.0 copy.64
  345.0 37.6 %while.14 = (s32[]{:T(128)}, bf16[4,512,256]{2,1,0:T(8,128)(2,1)S(1)}, s32[4]{0:T(128)S(1)}, bf16[2048,1,128]{2,0,1:T(8,128)(2,1)}, s32[2048]{0:T(1024)S(1)}, /*...) while((s32[]{:T(128)}, ...), condition=%wide.region_6.7_spmd, body=%wide.region_3.6_spmd.sunk | while | flops 829816832 | bytes 26538252 | solution.py:109
  345.0 0.6 dynamic_slice.80
  346.4 1.1 compare_and_fusion.3
  347.6 2.5 fusion.40
  350.1 1.7 fusion.41
  351.8 2.4 fusion.42
  354.4 0.6 dynamic_slice.80
  355.8 1.1 compare_and_fusion.3
  357.0 2.5 fusion.40
  359.5 1.7 fusion.41
  361.2 2.4 fusion.42
  363.8 0.6 dynamic_slice.80
  365.2 1.1 compare_and_fusion.3
  366.4 2.5 fusion.40
  368.9 1.7 fusion.41
  370.6 2.4 fusion.42
  373.2 0.6 dynamic_slice.80
  374.6 1.1 compare_and_fusion.3
  375.8 2.5 fusion.40
  378.3 1.7 fusion.41
  380.0 2.4 fusion.42
  382.6 1.0 copy-done.4
  383.6 3.2 copy.92
  386.8 10.6 %reduce.19 = bf16[2048,256]{1,0:T(8,128)(2,1)S(1)} reduce(bf16[2048,1,256]{2,1,0:T(2,128)(2,1)S(1)} %bitcast.130, bf16[]{:T(256)} %broadcast.95), dimensions={1}, to_apply=%bitcast.104.reduce_sub_computation | reduce | bytes 2097154
  397.3 0.3 reshape.214
  397.6 20.7 %all_to_all.63 = bf16[16,2,16384]{2,1,0:T(2,128)(2,1)} all-to-all(bf16[16,2,16384]{2,1,0:T(2,128)(2,1)S(1)} %reshape.214), channel_id=1, replica_groups=mesh['fsdp'=16,'seq'=16] {'seq'}, dimensions={0} | all-to-all | bytes 2097152 | tf_op jit(solution)/shard_map/all_to_all | solution.py:112
  418.4 4.3 reshape.215
  422.7 1.1 copy.87
  423.8 1.6 copy.75
  425.4 1.1 convolution_convert_fusion
  426.5 1.3 copy.77
  427.8 58.0 %reduce-scatter.2.cloned.1.call-done = bf16[16,256]{1,0:T(8,128)(2,1)} async-done(((bf16[16,4096]{1,0:T(8,128)(2,1)}), bf16[16,256]{1,0:T(8,128)(2,1)}) %reduce-scatter.2.cloned.1.call-update) | async-done | bytes 8208 | tf_op jit(solution)/shard_map/reduce_scatter | solution.py:119
  485.9 1.4 divide_bitcast_fusion
  (69 shorter events, 2.5 us)
Async XLA Ops:
  7.2 260.8 %copy-start = (bf16[1,128,5120]{2,1,0:T(8,128)(2,1)S(1)}, bf16[1,128,5120]{2,1,0:T(8,128)(2,1)}, u32[]{:S(2)}) copy-start(bf16[1,128,5120]{2,1,0:T(8,128)(2,1)} %param.7) | copy-start | bytes 3932164
  7.2 38.1 %copy-start.6 = (s32[1,16]{1,0:T(1,128)S(1)}, s32[1,16]{1,0:T(1,128)}, u32[]{:S(2)}) copy-start(s32[1,16]{1,0:T(1,128)} %param.10) | copy-start | bytes 196
  7.2 38.3 %copy-start.8 = (s32[1,16]{1,0:T(1,128)S(1)}, s32[1,16]{1,0:T(1,128)}, u32[]{:S(2)}) copy-start(s32[1,16]{1,0:T(1,128)} %param.11) | copy-start | bytes 196
  7.2 260.8 %all-gather.2.cloned.1.call-start = ((), (), s32[]{:S(2)}) async-start(), calls=%async_computation.5 | async-start | bytes 22282240 | tf_op jit(solution)/shard_map/all_gather | solution.py:51
  39.0 260.8 %all-to-all-start.2 = ((bf16[16,2,16384]{2,1,0:T(2,128)(2,1)}), bf16[16,2,16384]{2,1,0:T(2,128)(2,1)S(1)}, u32[]{:S(2)}, u32[]{:S(2)}) async-start(bf16[16,2,16384]{2,1,0:T(2,128)(2,1)} %reshape.212), calls=%async_computation.2 | async-start | bytes 2097152 | tf_op jit(solution)/shard_map/all_to_all | solution.py:72
  299.8 31.3 %copy-start.2 = (bf16[16,2,16384]{2,1,0:T(2,128)(2,1)}, bf16[16,2,16384]{2,1,0:T(2,128)(2,1)S(1)}, u32[]{:S(2)}) copy-start(bf16[16,2,16384]{2,1,0:T(2,128)(2,1)S(1)} %all-to-all-done.2) | copy-start | bytes 3145732
  299.8 25.3 %all-to-all-start.1 = ((bf16[16,2,8192]{2,1,0:T(2,128)(2,1)}), bf16[16,2,8192]{2,1,0:T(2,128)(2,1)}, u32[]{:S(2)}, u32[]{:S(2)}) async-start(bf16[16,2,8192]{2,1,0:T(2,128)(2,1)} %reshape.210), calls=%async_computation.1 | async-start | bytes 1048576 | tf_op jit(solution)/shard_map/all_to_all | solution.py:73
  325.2 16.5 %all-to-all-start = ((bf16[16,2,8192]{2,1,0:T(2,128)(2,1)}), bf16[16,2,8192]{2,1,0:T(2,128)(2,1)}, u32[]{:S(2)}, u32[]{:S(2)}) async-start(bf16[16,2,8192]{2,1,0:T(2,128)(2,1)} %reshape.208), calls=%async_computation | async-start | bytes 1048576 | tf_op jit(solution)/shard_map/all_to_all | solution.py:74
  330.8 155.1 %reduce-scatter.2.cloned.1.call-start = ((), (), s32[]{:S(2)}) async-start(), calls=%async_computation.6 | async-start | bytes 139264 | tf_op jit(solution)/shard_map/reduce_scatter | solution.py:119
  335.6 9.4 %copy-start.3 = (bf16[4,512,256]{2,1,0:T(8,128)(2,1)S(1)}, bf16[4,512,256]{2,1,0:T(8,128)(2,1)}, u32[]{:S(2)}) copy-start(bf16[4,512,256]{2,1,0:T(8,128)(2,1)} %custom-call) | copy-start | bytes 3145732
  347.6 4.2 copy-start.5
  357.0 4.2 copy-start.5
  366.4 4.2 copy-start.5
  375.8 4.2 copy-start.5
  382.6 1.0 copy-start.4
  397.6 89.6 %copy-start.1 = (bf16[1,128,5120]{2,1,0:T(8,128)(2,1)S(1)}, bf16[1,128,5120]{2,1,0:T(8,128)(2,1)}, u32[]{:S(2)}) copy-start(bf16[1,128,5120]{2,1,0:T(8,128)(2,1)} %param.7) | copy-start | bytes 3932164
  418.4 67.5 %copy-start.7 = (f32[16]{0:T(128)S(1)}, f32[16]{0:T(128)}, u32[]{:S(2)}) copy-start(f32[16]{0:T(128)} %get-tuple-element.205) | copy-start | bytes 196
Sparse Core Ops, SparseCore 0:
  10.5 257.4 all-gather.1
  426.6 59.1 reduce-scatter.1
where the time goes:
time: 500 us; the launch traced here: 494 us
  waiting for transfers between devices  282 us (56%)
  other arithmetic  72.2 us (14%)
  local copies, waits for them, and re-layouts  56.5 us (11%)
  matrix products  29.2 us (6%)
  blocking collectives  20.7 us (4%)
  starting transfers between devices  16.6 us (3%)
  between operations  14.6 us (3%)
    all_gather x1, waiting for transfers between devices, on_device(): lax.all_gather(key_value_weight, 'fsdp', axis=0, tiled=True)  221 us
    reduce_scatter x1, waiting for transfers between devices, on_device(): lax.psum_scatter(partial_value.astype(jnp.bfloat16), 'seq', scatter_dimen...  58 us
    unnamed x4, other arithmetic  57.8 us
    unnamed x33, local copies, waits for them, and re-layouts  27.8 us
    all_to_all x1, blocking collectives, on_device(): lax.all_to_all(attn_heads[None], 'seq', split_axis=1, concat_axis=2, tile...  20.7 us
  transfers between devices with their start and end apart: 5, of which 3 were waited for; matrix products, arithmetic and copies ran while one was open for 19% of the time, Pallas kernels for 0%

commit v1 on v0

--- a/solution.py
+++ b/solution.py
@@ -48,7 +48,10 @@
     features = hidden[0]
     projected_rows = jnp.dot(
         features,
-        lax.all_gather(key_value_weight, "fsdp", axis=0, tiled=True),
+        jnp.concatenate(
+            lax.all_to_all(jnp.stack([key_value_weight] * lax.axis_size("fsdp")), "fsdp", 0, 0),
+            axis=0,
+        ),
         preferred_element_type=jnp.float32,
     )
     local_tables = token_tables(lengths, wanted, rank * token_batch, token_batch)

time: 500 us -> 770 us (1.54)
  waiting for transfers between devices: 282 us -> 527 us
  starting transfers between devices: 16.6 us -> 34 us
  local copies, waits for them, and re-layouts: 56.5 us -> 64.8 us
    all_to_all x0 -> x1, waiting for transfers between devices: none -> 425 us  [on_device(): lax.all_to_all(jnp.stack([key_value_weight] * lax.axis_size('fsdp')), 'fs...]
    all_gather x1 -> x0, waiting for transfers between devices: 221 us -> none  [on_device(): lax.all_gather(key_value_weight, 'fsdp', axis=0, tiled=True)]
    reduce_scatter x1, waiting for transfers between devices: 58 us -> 100 us  [on_device(): lax.psum_scatter(partial_value.astype(jnp.bfloat16), 'seq', scatter_dimen...]
    all_to_all x0 -> x1, starting transfers between devices: none -> 11.7 us  [on_device(): lax.all_to_all(jnp.stack([key_value_weight] * lax.axis_size('fsdp')), 'fs...]
    another operation x0 -> x1, local copies, waits for them, and re-layouts: none -> 8.34 us  [on_device(): jnp.stack([key_value_weight] * lax.axis_size('fsdp'))]
    unnamed x33 -> x31, local copies, waits for them, and re-layouts: 27.8 us -> 27.8 us
  transfers between devices with their start and end apart: 5 -> 5, of which waited for: 3 -> 3; matrix products, arithmetic and copies ran while one was open for 19% -> 12% of each run, Pallas kernels for 0% -> 0%
where the time goes in v1:
time: 770 us; the launch traced here: 764 us
  waiting for transfers between devices  527 us (68%)
  other arithmetic  71.4 us (9%)
  local copies, waits for them, and re-layouts  64.8 us (8%)
  starting transfers between devices  34 us (4%)
  matrix products  29.2 us (4%)
  blocking collectives  20.7 us (3%)
  between operations  14.6 us (2%)
    all_to_all x1, waiting for transfers between devices, on_device(): lax.all_to_all(jnp.stack([key_value_weight] * lax.axis_size('fsdp')), 'fs...  425 us
    reduce_scatter x1, waiting for transfers between devices, on_device(): lax.psum_scatter(partial_value.astype(jnp.bfloat16), 'seq', scatter_dimen...  100 us
    unnamed x4, other arithmetic  57.5 us
    unnamed x31, local copies, waits for them, and re-layouts  27.8 us
    all_to_all x1, blocking collectives, on_device(): lax.all_to_all(attn_heads[None], 'seq', split_axis=1, concat_axis=2, tile...  20.7 us
  transfers between devices with their start and end apart: 5, of which 3 were waited for; matrix products, arithmetic and copies ran while one was open for 12% of the time, Pallas kernels for 0%

profile of v1, /device:TPU:8, one launch (start us, length us, event | category | flops | bytes accessed | tf_op | source)
XLA Modules:
  0.0 764.5 jit_solution(11425218029641732076)
XLA Ops:
  7.2 8.3 %stack.2 = bf16[16,320,2048]{2,1,0:T(8,128)(2,1)} broadcast(bf16[320,2048]{1,0:T(8,128)(2,1)} %param.9), dimensions={1,2} | broadcast | bytes 22282240 | tf_op jit(solution)/shard_map/stack | solution.py:52
  15.5 11.7 %all-to-all-start = ((bf16[16,320,2048]{2,1,0:T(8,128)(2,1)}), bf16[16,320,2048]{2,1,0:T(8,128)(2,1)}, u32[]{:S(2)}, u32[]{:S(2)}) async-start(bf16[16,320,2048]{2,1,0:T(8,128)(2,1)} %stack.2), calls=%async_computation | async-start | bytes 41943040 | tf_op jit(solution)/shard_map/all_to_all | solution.py:52
  27.6 5.0 copy.69
  32.6 0.5 broadcast.97
  33.2 23.3 %reduce.18 = bf16[4096,128]{1,0:T(8,128)(2,1)} reduce(bf16[4096,1,128]{2,1,0:T(2,128)(2,1)S(1)} %bitcast.130, bf16[]{:T(256)} %broadcast.97), dimensions={1}, to_apply=%bitcast.92.reduce_sub_computation | reduce | bytes 2097154
  56.4 2.1 reshape.218
  58.6 425.4 %all-to-all-done = bf16[16,320,2048]{2,1,0:T(8,128)(2,1)} async-done(((bf16[16,320,2048]{2,1,0:T(8,128)(2,1)}), bf16[16,320,2048]{2,1,0:T(8,128)(2,1)}, u32[]{:S(2)}, u32[]{:S(2)}) %all-to-all-start) | async-done | bytes 20971552 | tf_op jit(solution)/shard_map/all_to_all | solution.py:52
  484.0 10.2 %all-to-all-start.3 = ((bf16[16,2,16384]{2,1,0:T(2,128)(2,1)}), bf16[16,2,16384]{2,1,0:T(2,128)(2,1)S(1)}, u32[]{:S(2)}, u32[]{:S(2)}) async-start(bf16[16,2,16384]{2,1,0:T(2,128)(2,1)} %reshape.218), calls=%async_computation.3 | async-start | bytes 2097152 | tf_op jit(solution)/shard_map/all_to_all | solution.py:75
  494.2 0.3 multiply_cosine_fusion
  494.5 8.5 %fusion.19 = f32[128,2048]{1,0:T(8,128)S(1)} fusion(bf16[5120,2048]{1,0:T(8,128)(2,1)} %bitcast.13, bf16[1,128,5120]{2,1,0:T(8,128)(2,1)S(1)} %copy-done), kind=kOutput, calls=%fused_computation.25 | convolution fusion | flops 2684354560 | bytes 23330816 | tf_op jit(solution)/shard_map/dot_general | solution.py:49
  503.2 0.3 subtract_convert_fusion
  503.4 0.1 pad_maximum_fusion
  503.6 0.2 copy.66
  503.9 8.1 %copy.93 = bf16[1,128,2048]{1,0,2:T(2,128)(2,1)S(1)} copy(bf16[1,128,2048]{1,2,0:T(8,128)(2,1)S(1)} %bitcast.140) | data formatting | bytes 1048576 | tf_op jit(solution)/shard_map/reshape | solution.py:70
  512.1 12.2 %reduce.17 = bf16[2048,128]{1,0:T(8,128)(2,1)} reduce(bf16[2048,1,128]{2,1,0:T(2,128)(2,1)S(1)} %bitcast.138, bf16[]{:T(256)} %broadcast.97), dimensions={1}, to_apply=%bitcast.106.reduce_sub_computation | reduce | bytes 1048578
  524.3 2.0 reshape.216
  526.3 6.0 all-to-all-start.2
  532.4 0.2 copy.79
  532.7 8.1 %copy.94 = bf16[1,128,2048]{1,0,2:T(2,128)(2,1)S(1)} copy(bf16[1,128,2048]{1,2,0:T(8,128)(2,1)S(1)} %bitcast.141) | data formatting | bytes 1048576 | tf_op jit(solution)/shard_map/reshape | solution.py:73
  540.8 11.5 %reduce.16 = bf16[2048,128]{1,0:T(8,128)(2,1)S(1)} reduce(bf16[2048,1,128]{2,1,0:T(2,128)(2,1)S(1)} %bitcast.139, bf16[]{:T(256)} %broadcast.97), dimensions={1}, to_apply=%bitcast.107.reduce_sub_computation | reduce | bytes 1048578
  552.3 0.9 reshape.214
  553.2 5.9 all-to-all-start.1
  559.1 0.3 reduce-scatter.2.cloned.1.call-start
  559.4 4.3 reshape.219
  563.9 0.7 copy.70
  564.6 1.3 reshape_squeeze.11
  565.9 2.2 reshape.217
  568.2 0.3 copy.68
  568.5 1.5 all-to-all-done.1
  569.9 2.2 reshape.215
  572.2 1.0 copy.64
  573.3 37.5 %while.14 = (s32[]{:T(128)}, bf16[4,512,256]{2,1,0:T(8,128)(2,1)S(1)}, s32[4]{0:T(128)S(1)}, bf16[2048,1,128]{2,0,1:T(8,128)(2,1)}, s32[2048]{0:T(1024)S(1)}, /*...) while((s32[]{:T(128)}, ...), condition=%wide.region_6.7_spmd, body=%wide.region_3.6_spmd.sunk | while | flops 829816832 | bytes 26538244 | solution.py:112
  573.3 0.6 dynamic_slice.80
  574.7 1.2 compare_and_fusion.3
  575.9 2.5 fusion.40
  578.4 1.7 fusion.41
  580.1 2.4 fusion.42
  582.7 0.6 dynamic_slice.80
  584.1 1.2 compare_and_fusion.3
  585.2 2.5 fusion.40
  587.8 1.7 fusion.41
  589.4 2.4 fusion.42
  592.1 0.6 dynamic_slice.80
  593.5 1.2 compare_and_fusion.3
  594.6 2.5 fusion.40
  597.1 1.7 fusion.41
  598.8 2.4 fusion.42
  601.4 0.6 dynamic_slice.80
  602.9 1.2 compare_and_fusion.3
  604.0 2.5 fusion.40
  606.5 1.7 fusion.41
  608.2 2.4 fusion.42
  610.8 1.0 copy-done.4
  611.8 3.2 copy.92
  615.0 10.5 %reduce.19 = bf16[2048,256]{1,0:T(8,128)(2,1)S(1)} reduce(bf16[2048,1,256]{2,1,0:T(2,128)(2,1)S(1)} %bitcast.131, bf16[]{:T(256)} %broadcast.97), dimensions={1}, to_apply=%bitcast.105.reduce_sub_computation | reduce | bytes 2097154
  625.5 0.3 reshape.220
  625.8 20.7 %all_to_all.68 = bf16[16,2,16384]{2,1,0:T(2,128)(2,1)} all-to-all(bf16[16,2,16384]{2,1,0:T(2,128)(2,1)S(1)} %reshape.220), channel_id=1, replica_groups=mesh['fsdp'=16,'seq'=16] {'seq'}, dimensions={0} | all-to-all | bytes 2097152 | tf_op jit(solution)/shard_map/all_to_all | solution.py:115
  646.5 4.3 reshape.221
  650.8 1.1 copy.87
  652.0 1.6 copy.75
  653.6 1.1 convolution_convert_fusion
  654.7 1.3 copy.77
  656.0 100.0 %reduce-scatter.2.cloned.1.call-done = bf16[16,256]{1,0:T(8,128)(2,1)} async-done(((bf16[16,4096]{1,0:T(8,128)(2,1)}), bf16[16,256]{1,0:T(8,128)(2,1)}) %reduce-scatter.2.cloned.1.call-update) | async-done | bytes 8208 | tf_op jit(solution)/shard_map/reduce_scatter | solution.py:122
  756.0 1.4 divide_bitcast_fusion
  (67 shorter events, 2.4 us)
Async XLA Ops:
  7.2 487.3 %copy-start = (bf16[1,128,5120]{2,1,0:T(8,128)(2,1)S(1)}, bf16[1,128,5120]{2,1,0:T(8,128)(2,1)}, u32[]{:S(2)}) copy-start(bf16[1,128,5120]{2,1,0:T(8,128)(2,1)} %param.7) | copy-start | bytes 3932164
  15.5 11.7 %copy-start.6 = (s32[1,16]{1,0:T(1,128)S(1)}, s32[1,16]{1,0:T(1,128)}, u32[]{:S(2)}) copy-start(s32[1,16]{1,0:T(1,128)} %param.10) | copy-start | bytes 196
  15.5 11.9 %copy-start.7 = (s32[1,16]{1,0:T(1,128)S(1)}, s32[1,16]{1,0:T(1,128)}, u32[]{:S(2)}) copy-start(s32[1,16]{1,0:T(1,128)} %param.11) | copy-start | bytes 196
  15.5 468.4 %all-to-all-start = ((bf16[16,320,2048]{2,1,0:T(8,128)(2,1)}), bf16[16,320,2048]{2,1,0:T(8,128)(2,1)}, u32[]{:S(2)}, u32[]{:S(2)}) async-start(bf16[16,320,2048]{2,1,0:T(8,128)(2,1)} %stack.2), calls=%async_computation | async-start | bytes 41943040 | tf_op jit(solution)/shard_map/all_to_all | solution.py:52
  484.0 42.3 %all-to-all-start.3 = ((bf16[16,2,16384]{2,1,0:T(2,128)(2,1)}), bf16[16,2,16384]{2,1,0:T(2,128)(2,1)S(1)}, u32[]{:S(2)}, u32[]{:S(2)}) async-start(bf16[16,2,16384]{2,1,0:T(2,128)(2,1)} %reshape.218), calls=%async_computation.3 | async-start | bytes 2097152 | tf_op jit(solution)/shard_map/all_to_all | solution.py:75
  526.3 33.1 %copy-start.2 = (bf16[16,2,16384]{2,1,0:T(2,128)(2,1)}, bf16[16,2,16384]{2,1,0:T(2,128)(2,1)S(1)}, u32[]{:S(2)}) copy-start(bf16[16,2,16384]{2,1,0:T(2,128)(2,1)S(1)} %all-to-all-done.3) | copy-start | bytes 3145732
  526.3 26.9 %all-to-all-start.2 = ((bf16[16,2,8192]{2,1,0:T(2,128)(2,1)}), bf16[16,2,8192]{2,1,0:T(2,128)(2,1)}, u32[]{:S(2)}, u32[]{:S(2)}) async-start(bf16[16,2,8192]{2,1,0:T(2,128)(2,1)} %reshape.216), calls=%async_computation.2 | async-start | bytes 1048576 | tf_op jit(solution)/shard_map/all_to_all | solution.py:76
  553.2 16.7 %all-to-all-start.1 = ((bf16[16,2,8192]{2,1,0:T(2,128)(2,1)}), bf16[16,2,8192]{2,1,0:T(2,128)(2,1)}, u32[]{:S(2)}, u32[]{:S(2)}) async-start(bf16[16,2,8192]{2,1,0:T(2,128)(2,1)} %reshape.214), calls=%async_computation.1 | async-start | bytes 1048576 | tf_op jit(solution)/shard_map/all_to_all | solution.py:77
  559.1 196.9 %reduce-scatter.2.cloned.1.call-start = ((), (), s32[]{:S(2)}) async-start(), calls=%async_computation.6 | async-start | bytes 139264 | tf_op jit(solution)/shard_map/reduce_scatter | solution.py:122
  563.9 9.4 %copy-start.3 = (bf16[4,512,256]{2,1,0:T(8,128)(2,1)S(1)}, bf16[4,512,256]{2,1,0:T(8,128)(2,1)}, u32[]{:S(2)}) copy-start(bf16[4,512,256]{2,1,0:T(8,128)(2,1)} %custom-call) | copy-start | bytes 3145732
  575.8 4.2 copy-start.5
  585.2 4.2 copy-start.5
  594.6 4.2 copy-start.5
  604.0 4.2 copy-start.5
  610.8 1.0 copy-start.4
  625.8 131.6 %copy-start.1 = (bf16[1,128,5120]{2,1,0:T(8,128)(2,1)S(1)}, bf16[1,128,5120]{2,1,0:T(8,128)(2,1)}, u32[]{:S(2)}) copy-start(bf16[1,128,5120]{2,1,0:T(8,128)(2,1)} %param.7) | copy-start | bytes 3932164
Sparse Core Ops, SparseCore 0:
  654.8 101.1 reduce-scatter.1
